TPU v7x, 256 devices: a whole 4x4x8 slice. The times are simulated.
256 devices in a mesh: row: 16 (over x, y_lo, core), col: 16 (over z, y_hi).
Axes of the slice: x: 4, y: 4 (y_hi: 2, y_lo: 2; y = y_hi * 2 + y_lo), z: 8, core: 2. Of those that a mesh axis runs over, the one named last changes fastest.
Arguments:
- ancestor_inverse: float32 [24576, 24576], P('row', 'col'), may hold values from -1 to 5, as said below
- factor_panel: float32 [24576, 512], P('row'), may hold values from -6 to 6
- ancestor_blocks: int32 [16, 12], replicated, may hold values from 0 to 11, each once within a row
- ancestor_count: int32 [16], replicated, may hold values from 1 to 12, 128 in all
Outputs:
- inverse_panel: float32 [24576, 512], P(('row', 'col'))
- inverse_row: float32 [512, 24576], P('row', 'col')
Inputs may be any that keep to these rules, and one draw needn't show every extreme that they name: ancestor_inverse is symmetric: equal to its transpose. `ancestor_blocks`: each row is an ordering of the 12 blocks of one tile. `ancestor_count`: the counts sum to 128, and some tile has all 12 slots live.
All inputs are finite; a program needn't handle non-finite values.
Results may differ from a plain program's by a relative error of at most 0.000071.
Values sent between devices are 32-bit elements; how exact they have to be, the bound alone decides.
No kernel may reach another device: no remote copies, remote signals or barrier semaphores. Data moves between devices by JAX's collectives and lax.ppermute only.
A program may use at most 128 MiB of HBM per device.

v0:
```python
import jax
import jax.numpy as jnp
from jax import lax
from jax.sharding import PartitionSpec as P

highest = lax.Precision.HIGHEST


def from_root(value, axis, source):
    kept = jnp.where(lax.axis_index(axis) == source, value, 0).astype(value.dtype)
    return lax.psum(kept, axis)


def slot_table(row_order, row_count, tile_blocks):
    slot_ids = lax.iota(jnp.int32, tile_blocks)
    active = slot_ids < row_count
    onehot = jnp.logical_and(row_order[:, None] == slot_ids[None, :], active[:, None])
    return (onehot.astype(jnp.float32), active)


def to_natural(panel_tile, onehot, block_rows):
    tile_blocks = onehot.shape[0]
    blocks = panel_tile.reshape(tile_blocks, block_rows, panel_tile.shape[1])
    placed = jnp.einsum("sj,sbw->jbw", onehot, blocks, precision=highest)
    return placed.reshape(tile_blocks * block_rows, panel_tile.shape[1])


def natural_index(row_order, active, block_rows, tile_start):
    within = lax.iota(jnp.int32, block_rows)
    positions = (tile_start + row_order[:, None] * block_rows + within[None, :]).reshape(-1)
    keep_mask = jnp.repeat(active.astype(jnp.float32), block_rows)
    return (positions, keep_mask)


def per_device(ancestor_inverse, factor_panel, ancestor_blocks, ancestor_count):
    row_devices = lax.axis_size("row")
    col_devices = lax.axis_size("col")
    per_column = row_devices // col_devices
    grid_row = lax.axis_index("row")
    grid_col = lax.axis_index("col")
    tile_rows = factor_panel.shape[0]
    super_width = factor_panel.shape[1]
    tile_blocks = ancestor_blocks.shape[1]
    block_rows = tile_rows // tile_blocks
    col_lists = []
    mask_lists = []
    source = grid_col * per_column + 0
    arrived = from_root(factor_panel, "row", source)
    row_order = lax.dynamic_index_in_dim(ancestor_blocks, source, 0, keepdims=False)
    row_count = lax.dynamic_index_in_dim(ancestor_count, source, 0, keepdims=False)
    onehot, active = slot_table(row_order, row_count, tile_blocks)
    panels = to_natural(arrived, onehot, block_rows)
    where_cols, keep_cols = natural_index(row_order, active, block_rows, 0)
    col_lists.append(where_cols)
    mask_lists.append(keep_cols)
    own_order = lax.dynamic_index_in_dim(ancestor_blocks, grid_row, 0, keepdims=False)
    own_count = lax.dynamic_index_in_dim(ancestor_count, grid_row, 0, keepdims=False)
    own_hot, own_active = slot_table(own_order, own_count, tile_blocks)
    row_positions, row_mask = natural_index(own_order, own_active, block_rows, 0)
    share_rows = tile_rows // col_devices
    picked = jnp.take(ancestor_inverse, row_positions, axis=0)
    product = jnp.dot(picked, panels, precision=highest, preferred_element_type=jnp.float32)
    inverse_panel = lax.psum_scatter(
        -product * row_mask[:, None], "col", scatter_dimension=0, tiled=True
    )
    moved = inverse_panel.T.reshape(super_width, 1, share_rows)
    mirrored = lax.all_to_all(
        lax.all_to_all(moved, "row", split_axis=0, concat_axis=1, tiled=True),
        "col",
        split_axis=1,
        concat_axis=2,
        tiled=True,
    )
    inverse_row = mirrored.reshape(super_width // row_devices, per_column * tile_rows)
    return (inverse_panel, inverse_row)


def solution(mesh):
    placed = (P("row", "col"), P("row", None), P(), P())
    return jax.shard_map(
        per_device,
        mesh=mesh,
        in_specs=placed,
        out_specs=(P(("row", "col"), None), P("row", "col")),
        check_vma=False,
    )
```

profile of v0, /device:TPU:1, one launch (start us, length us, event | category | flops | bytes accessed | tf_op | source)
XLA Modules:
  0.0 428.5 jit_solution(5537427536059488078)
XLA Ops:
  7.2 0.0 all-reduce.2.cloned.1.call-start
  7.2 0.4 broadcast_select_fusion
  7.6 3.8 copy.14
  11.4 0.0 all-reduce.2.cloned.1.call-update
  11.4 0.0 reduce-scatter.2.cloned.1.call-start
  11.5 0.8 multiply_bitcast_fusion
  12.2 0.1 fusion.10
  12.4 0.0 copy-start.1
  12.4 14.1 %gather_fusion = f32[1536,1536]{1,0:T(8,128)} fusion(f32[1536,1536]{1,0:T(8,128)} %param.4, s32[2048]{0:T(1024)S(1)} %pad_clamp_fusion), kind=kCustom, calls=%fused_computation | custom fusion | bytes 18880512 | tf_op jit(solution)/shard_map/jit(_take)/gather | solution.py:61
  26.5 0.0 copy-done.1
  26.5 0.6 fusion.22
  27.1 0.6 compare_convert_fusion
  27.7 0.7 iota_compare_fusion.1
  28.4 0.1 fusion.13
  28.5 0.1 broadcast_bitcast_fusion
  28.5 123.2 %all-reduce.2.cloned.1.call-done = f32[12,128,512]{2,0,1:T(8,128)} async-done(((f32[12,128,512]{2,0,1:T(8,128)}), f32[12,128,512]{2,0,1:T(8,128)}) %all-reduce.2.cloned.1.call-update) | async-done | bytes 3145744 | tf_op jit(solution)/shard_map/psum | solution.py:11
  151.7 0.0 copy-start
  151.7 4.4 %fusion.16 = f32[12,128,512]{2,0,1:T(8,128)S(1)} fusion(f32[12,128,512]{2,0,1:T(8,128)} %all-reduce.2.cloned.1.call-done, s32[12]{0:T(128)S(1)} %get-tuple-element.3, pred[12]{0:T(512)(128)(4,1)S(1)} %iota_compare_fusion.1), kind=kOutput, calls=%fused_computation.19 | convolution fusion | flops 113246496 | bytes 6291516 | tf_op jit(solution)/shard_map/sj,sbw->jbw/dot_general | solution.py:24
  156.2 1.8 copy.15
  158.0 0.0 copy-done
  158.0 17.1 %fusion.7 = f32[1536,512]{1,0:T(8,128)} fusion(f32[1536,512]{1,0:T(8,128)S(1)} %bitcast.40, f32[1536,1536]{1,0:T(8,128)S(1)} %copy-done, pred[1536]{0:T(1024)(128)(4,1)S(1)} %fusion.13, f32[1536]{0:T(1024)S(1)} %broadcast_bitcast_fusion), kind=kOutput, calls=%fused_computation.6 | convolution fusion | flops 14499446784 | bytes 15736320 | tf_op jit(solution)/shard_map/dot_general | solution.py:62
  175.2 0.0 reduce-scatter.2.cloned.1.call-update
  175.2 209.3 %reduce-scatter.2.cloned.1.call-done = f32[96,512]{1,0:T(8,128)} async-done(((f32[1536,512]{1,0:T(8,128)}), f32[96,512]{1,0:T(8,128)}) %reduce-scatter.2.cloned.1.call-update) | async-done | bytes 196624 | tf_op jit(solution)/shard_map/reduce_scatter | solution.py:63
  384.4 1.0 copy.16
  385.5 16.2 %all_to_all.27 = f32[512,1,96]{2,1,0:T(1,128)S(1)} all-to-all(f32[512,1,96]{2,1,0:T(1,128)S(1)} %copy.16), channel_id=1, replica_groups=mesh['row'=16,'col'=16] {'row'}, dimensions={0} | all-to-all | bytes 393216 | tf_op jit(solution)/shard_map/all_to_all | solution.py:68
  401.7 19.0 %all_to_all.28 = f32[32,16,96]{2,0,1:T(8,128)S(1)} all-to-all(f32[32,16,96]{2,0,1:T(8,128)S(1)} %bitcast.41), channel_id=1, replica_groups=mesh['row'=16,'col'=16] {'col'}, dimensions={1} | all-to-all | bytes 393216 | tf_op jit(solution)/shard_map/all_to_all | solution.py:67
  420.7 0.2 copy.17
  420.8 0.8 reshape.79
  (2 shorter events, 0.0 us)
Async XLA Ops:
  7.2 144.6 %all-reduce.2.cloned.1.call-start = ((), (), s32[]{:S(2)}) async-start(), calls=%async_computation.3 | async-start | bytes 8388608 | tf_op jit(solution)/shard_map/psum | solution.py:11
  11.4 373.0 %reduce-scatter.2.cloned.1.call-start = ((), (), s32[]{:S(2)}) async-start(), calls=%async_computation.4 | async-start | bytes 3342336 | tf_op jit(solution)/shard_map/reduce_scatter | solution.py:63
  12.4 14.1 %copy-start.1 = (s32[16]{0:T(128)S(1)}, s32[16]{0:T(128)}, u32[]{:S(2)}) copy-start(s32[16]{0:T(128)} %param.7) | copy-start | bytes 196
  151.7 6.3 %copy-start = (f32[1536,1536]{1,0:T(8,128)S(1)}, f32[1536,1536]{1,0:T(8,128)}, u32[]{:S(2)}) copy-start(f32[1536,1536]{1,0:T(8,128)} %gather_fusion) | copy-start | bytes 28311556
Sparse Core Ops, SparseCore 0:
  11.5 140.1 all-reduce.1
  175.3 209.0 reduce-scatter.1
where the time goes:
time: 429 us; the launch traced here: 428 us
  waiting for transfers between devices  333 us (78%)
  blocking collectives  35.2 us (8%)
  local copies, waits for them, and re-layouts  22.4 us (5%)
  matrix products  21.6 us (5%)
  between operations  14.1 us (3%)
    reduce_scatter x1, waiting for transfers between devices, per_device(): lax.psum_scatter(-product * row_mask[:, None], 'col', scatter_dimension=0...  209 us
    psum x1, waiting for transfers between devices, from_root(): return lax.psum(kept, axis)  123 us
    all_to_all x1, blocking collectives, per_device(): lax.all_to_all(lax.all_to_all(moved, 'row', split_axis=0, concat_axis=1,...  19 us
    dot_general x1, matrix products, per_device(): jnp.dot(picked, panels, precision=highest, preferred_element_type=jnp.flo...  17.1 us
    all_to_all x1, blocking collectives, per_device(): lax.all_to_all(moved, 'row', split_axis=0, concat_axis=1, tiled=True)  16.2 us
    gather x1, local copies, waits for them, and re-layouts, per_device(): picked = jnp.take(ancestor_inverse, row_positions, axis=0)  14.1 us
  transfers between devices with their start and end apart: 2, of which 2 were waited for; matrix products, arithmetic and copies ran while one was open for 4% of the time, Pallas kernels for 0%

commit v1 on v0

--- a/solution.py
+++ b/solution.py
@@ -6,9 +6,15 @@
 highest = lax.Precision.HIGHEST
 
 
+def summed_here(block, axis):
+    pieces = lax.all_gather(block, axis, axis=0, tiled=False)
+    total = pieces.sum(axis=0)
+    return total
+
+
 def from_root(value, axis, source):
     kept = jnp.where(lax.axis_index(axis) == source, value, 0).astype(value.dtype)
-    return lax.psum(kept, axis)
+    return summed_here(kept, axis)
 
 
 def slot_table(row_order, row_count, tile_blocks):

time: 429 us -> 561 us (1.31)
  waiting for transfers between devices: 333 us -> 449 us
  other arithmetic: 2.63 us -> 22.8 us
    all_gather x0 -> x1, waiting for transfers between devices: none -> 241 us  [summed_here(): pieces = lax.all_gather(block, axis, axis=0, tiled=False)]
    psum x1 -> x0, waiting for transfers between devices: 123 us -> none  [from_root(): return lax.psum(kept, axis)]
    reduce_sum x0 -> x1, other arithmetic: none -> 18.6 us  [summed_here(): total = pieces.sum(axis=0)]
  transfers between devices with their start and end apart: 2 -> 2, of which waited for: 2 -> 2; matrix products, arithmetic and copies ran while one was open for 4% -> 3% of each run, Pallas kernels for 0% -> 0%
where the time goes in v1:
time: 561 us
  waiting for transfers between devices  449 us (80%)
  blocking collectives  35.3 us (6%)
  other arithmetic  22.8 us (4%)
  matrix products  21.1 us (4%)
  local copies, waits for them, and re-layouts  18.5 us (3%)
  between operations  14.1 us (3%)
    all_gather x1, waiting for transfers between devices, summed_here(): pieces = lax.all_gather(block, axis, axis=0, tiled=False)  241 us
    reduce_scatter x1, waiting for transfers between devices, per_device(): lax.psum_scatter(-product * row_mask[:, None], 'col', scatter_dimension=0...  208 us
    all_to_all x1, blocking collectives, per_device(): lax.all_to_all(lax.all_to_all(moved, 'row', split_axis=0, concat_axis=1,...  19.1 us
    reduce_sum x1, other arithmetic, summed_here(): total = pieces.sum(axis=0)  18.6 us
    dot_general x1, matrix products, per_device(): jnp.dot(picked, panels, precision=highest, preferred_element_type=jnp.flo...  17.2 us
    all_to_all x1, blocking collectives, per_device(): lax.all_to_all(moved, 'row', split_axis=0, concat_axis=1, tiled=True)  16.1 us
    gather x1, local copies, waits for them, and re-layouts, per_device(): picked = jnp.take(ancestor_inverse, row_positions, axis=0)  14 us
  transfers between devices with their start and end apart: 2, of which 2 were waited for; matrix products, arithmetic and copies ran while one was open for 3% of the time, Pallas kernels for 0%

profile of v1, /device:TPU:1, one launch (start us, length us, event | category | flops | bytes accessed | tf_op | source)
XLA Modules:
  0.0 560.8 jit_solution(15582330299241973841)
XLA Ops:
  7.2 0.0 all-gather.3.cloned.1.call-start
  7.2 2.0 broadcast_select_fusion
  9.2 0.0 all-gather.3.cloned.1.call-update
  9.2 0.0 reduce-scatter.2.cloned.1.call-start
  9.3 0.8 multiply_bitcast_fusion
  10.0 0.1 fusion.12
  10.2 0.0 copy-start.1
  10.2 14.0 %gather_fusion = f32[1536,1536]{1,0:T(8,128)} fusion(f32[1536,1536]{1,0:T(8,128)} %param.4, s32[2048]{0:T(1024)S(1)} %pad_clamp_fusion), kind=kCustom, calls=%fused_computation | custom fusion | bytes 18880512 | tf_op jit(solution)/shard_map/jit(_take)/gather | solution.py:67
  24.2 0.0 copy-done.1
  24.2 0.6 fusion.23
  24.8 0.6 iota_compare_fusion.1
  25.5 0.7 compare_convert_fusion
  26.1 0.1 fusion.15
  26.2 0.1 broadcast_bitcast_fusion
  26.3 240.8 %all-gather.3.cloned.1.call-done = f32[24576,512]{1,0:T(8,128)} async-done(((f32[1536,512]{1,0:T(8,128)}), f32[24576,512]{1,0:T(8,128)}) %all-gather.3.cloned.1.call-update) | async-done | bytes 50331664 | tf_op jit(solution)/shard_map/all_gather | solution.py:10
  267.1 18.6 %reduce_sum.9 = f32[1536,512]{1,0:T(8,128)S(1)} reduce(f32[16,1536,512]{2,1,0:T(8,128)} %bitcast.39, f32[]{:T(128)} %constant.41.clone.1), dimensions={0}, to_apply=%region_0.1 | reduce | flops 11796480 | bytes 53477380 | tf_op jit(solution)/shard_map/reduce_sum | solution.py:11
  285.7 0.0 copy-start
  285.7 3.9 fusion.4
  289.5 1.8 copy.15
  291.4 0.0 copy-done
  291.4 17.2 %fusion.9 = f32[1536,512]{1,0:T(8,128)} fusion(f32[1536,512]{1,0:T(8,128)S(1)} %bitcast.41, f32[1536,1536]{1,0:T(8,128)S(1)} %copy-done, pred[1536]{0:T(1024)(128)(4,1)S(1)} %fusion.15, f32[1536]{0:T(1024)S(1)} %broadcast_bitcast_fusion), kind=kOutput, calls=%fused_computation.8 | convolution fusion | flops 14499446784 | bytes 15736320 | tf_op jit(solution)/shard_map/dot_general | solution.py:68
  308.6 0.0 reduce-scatter.2.cloned.1.call-update
  308.6 208.1 %reduce-scatter.2.cloned.1.call-done = f32[96,512]{1,0:T(8,128)} async-done(((f32[1536,512]{1,0:T(8,128)}), f32[96,512]{1,0:T(8,128)}) %reduce-scatter.2.cloned.1.call-update) | async-done | bytes 196624 | tf_op jit(solution)/shard_map/reduce_scatter | solution.py:69
  516.7 1.0 copy.16
  517.7 16.1 %all_to_all.27 = f32[512,1,96]{2,1,0:T(1,128)S(1)} all-to-all(f32[512,1,96]{2,1,0:T(1,128)S(1)} %copy.16), channel_id=1, replica_groups=mesh['row'=16,'col'=16] {'row'}, dimensions={0} | all-to-all | bytes 393216 | tf_op jit(solution)/shard_map/all_to_all | solution.py:74
  533.9 19.1 %all_to_all.28 = f32[32,16,96]{2,0,1:T(8,128)S(1)} all-to-all(f32[32,16,96]{2,0,1:T(8,128)S(1)} %bitcast.42), channel_id=1, replica_groups=mesh['row'=16,'col'=16] {'col'}, dimensions={1} | all-to-all | bytes 393216 | tf_op jit(solution)/shard_map/all_to_all | solution.py:73
  553.0 0.2 copy.17
  553.2 0.8 reshape.79
  (2 shorter events, 0.0 us)
Async XLA Ops:
  7.2 259.9 %all-gather.3.cloned.1.call-start = ((), (), s32[]{:S(2)}) async-start(), calls=%async_computation.4 | async-start | bytes 53477376 | tf_op jit(solution)/shard_map/all_gather | solution.py:10
  9.2 507.5 %reduce-scatter.2.cloned.1.call-start = ((), (), s32[]{:S(2)}) async-start(), calls=%async_computation.3 | async-start | bytes 3342336 | tf_op jit(solution)/shard_map/reduce_scatter | solution.py:69
  10.2 14.0 %copy-start.1 = (s32[16]{0:T(128)S(1)}, s32[16]{0:T(128)}, u32[]{:S(2)}) copy-start(s32[16]{0:T(128)} %param.7) | copy-start | bytes 196
  285.7 5.7 %copy-start = (f32[1536,1536]{1,0:T(8,128)S(1)}, f32[1536,1536]{1,0:T(8,128)}, u32[]{:S(2)}) copy-start(f32[1536,1536]{1,0:T(8,128)} %gather_fusion) | copy-start | bytes 28311556
Sparse Core Ops, SparseCore 0:
  9.8 257.2 all-gather.2
  308.7 207.8 reduce-scatter.1
